TPU v7x, 32 devices: a whole 2x2x4 slice. The times are simulated.
32 devices in a mesh: groups: 2 (over y), dp: 2 (over x), expert: 8 (over z, core).
Axes of the slice: x: 2, y: 2, z: 4, core: 2. Of those that a mesh axis runs over, the one named last changes fastest.
Arguments:
- tokens: bfloat16 [4096, 2048], P(('groups', 'dp', 'expert')), parts along dimension 0, may hold values from -6 to 6
- routes: int32 [4096, 4], P(('groups', 'dp', 'expert')), parts along dimension 0, may hold values from 0 to 7, all different within a row; in each aligned block of 128 rows (0 to 127, 128 to 255, ...) at most 128 rows name the same one
- w_gate: bfloat16 [16, 2048, 512], P(('groups', 'expert')), parts along dimension 0, may hold values from -0.125 to 0.125
- w_up: bfloat16 [16, 2048, 512], P(('groups', 'expert')), parts along dimension 0, may hold values from -0.125 to 0.125
Outputs:
- r_factor: float32 [16, 512, 512], P(('groups', 'expert'), 'dp'), parts along dimension 0
There are 2 independent parts, one for each index of `groups`. A program takes and returns all parts, laid end to end along the dimension named above; each array names one. Nothing has to cross between parts.
Inputs may be any that keep to these rules, and one draw needn't show every extreme that they name: `routes`: each row names 4 different experts. In each aligned block of 128 rows (the tokens of one device) no expert is named by more than 128 rows, and in some block some expert is named by exactly 128 rows.
All inputs are finite; a program needn't handle non-finite values.
Results may differ from a plain program's by a relative error of at most 0.0027.
Values may be sent and summed in bfloat16 or wider, within the bound.
No kernel may reach another device: no remote copies, remote signals or barrier semaphores. Data moves between devices by JAX's collectives and lax.ppermute only.
A program may use at most 64 MiB of HBM per device.

v0:
```python
import jax
import jax.numpy as jnp
from jax import lax
from jax.sharding import PartitionSpec as P

RIDGE = 0.05


def body(tokens, routes, w_gate, w_up):
    owners = lax.axis_size("expert")
    data_ranks = lax.axis_size("dp")
    experts = w_gate.shape[0] * owners
    factor_width = w_gate.shape[2]
    model_width = tokens.shape[1]
    tok_rows, top_count = routes.shape
    capacity = min(tok_rows, 2 * tok_rows * top_count // experts)
    assigned = routes.reshape(-1)
    onehot = (assigned[:, None] == jnp.arange(experts, dtype=jnp.int32)[None, :]).astype(jnp.int32)
    position = jnp.sum(jnp.cumsum(onehot, axis=0) * onehot, axis=1) - 1
    target = assigned * capacity + position
    anchor = jnp.arange(tok_rows * top_count, dtype=jnp.int32) // top_count
    source_row = jnp.zeros((experts * capacity,), jnp.int32).at[target].set(anchor)
    filled = jnp.zeros((experts * capacity,), jnp.int32).at[target].set(1)
    outbox = jnp.where(filled[:, None] > 0, tokens[source_row], jnp.zeros((), tokens.dtype))
    outbox = outbox.reshape(experts, capacity, model_width)
    gate_matrix = w_gate[0]
    up_matrix = w_up[0]
    arrived = lax.all_to_all(outbox, "expert", split_axis=0, concat_axis=0, tiled=True)
    flattened = arrived.reshape(-1, model_width)
    gate_proj = jnp.dot(flattened, gate_matrix, preferred_element_type=jnp.float32)
    up_proj = jnp.dot(flattened, up_matrix, preferred_element_type=jnp.float32)
    hidden = (jax.nn.silu(gate_proj) * up_proj).astype(jnp.bfloat16)
    hidden = hidden.reshape(arrived.shape[0], arrived.shape[1], factor_width)
    hidden = hidden.reshape(-1, factor_width)
    gram_local = lax.dot_general(
        hidden, hidden, (((0,), (0,)), ((), ())), preferred_element_type=jnp.float32
    )
    rows_mean = data_ranks * tok_rows * top_count
    block_rows = factor_width // data_ranks
    my_rank = lax.axis_index("dp")
    summed = lax.psum(gram_local, "dp")
    regular = summed / rows_mean + RIDGE * jnp.eye(factor_width, dtype=jnp.float32)
    factor = jnp.linalg.cholesky(regular).T
    my_rows = lax.dynamic_slice_in_dim(factor, my_rank * block_rows, block_rows, 0)
    return my_rows.reshape(1, block_rows, factor_width)


def solution(mesh):
    in_specs = (
        P(("groups", "dp", "expert"), None),
        P(("groups", "dp", "expert"), None),
        P(("groups", "expert"), None, None),
        P(("groups", "expert"), None, None),
    )
    out_specs = P(("groups", "expert"), "dp", None)
    return jax.shard_map(body, mesh=mesh, in_specs=in_specs, out_specs=out_specs, check_vma=False)
```

profile of v0, /device:TPU:0, one launch (start us, length us, event | category | flops | bytes accessed | tf_op | source)
XLA Modules:
  0.0 292.4 jit_solution(2657920740436624957)
XLA Ops:
  6.5 0.9 copy.15
  8.4 1.1 reduce-window.6
  10.1 2.4 scatter_custom_fusion.1
  12.6 2.4 scatter_custom_fusion
  15.1 9.9 %gather_fusion = bf16[1024,2048]{1,0:T(8,128)(2,1)} fusion(bf16[128,2048]{1,0:T(8,128)(2,1)} %param.4, s32[1024]{0:T(1024)S(1)} %fusion.26), kind=kCustom, calls=%fused_computation | custom fusion | bytes 8392704 | tf_op jit(solution)/shard_map/gather | solution.py:24
  25.0 2.5 broadcast_select_fusion
  27.6 100.1 %all_to_all.5 = bf16[8,128,2048]{2,1,0:T(8,128)(2,1)S(1)} all-to-all(bf16[8,128,2048]{2,1,0:T(8,128)(2,1)S(1)} %broadcast_select_fusion), channel_id=1, replica_groups=mesh['groups'=2,'dp'=2,'expert'=8] {'expert'}, dimensions={0} | all-to-all | bytes 8388608 | tf_op jit(solution)/shard_map/all_to_all | solution.py:28
  127.7 1.9 copy-done.2
  129.6 3.7 %fusion = f32[1024,512]{1,0:T(8,128)} fusion(bf16[1024,2048]{1,0:T(8,128)(2,1)S(1)} %bitcast.49, bf16[1,2048,512]{2,1,0:T(8,128)(2,1)S(1)} %copy-done), kind=kOutput, calls=%fused_computation.4 | convolution fusion | flops 2147483648 | bytes 8388608 | tf_op jit(solution)/shard_map/dot_general | solution.py:31
  133.3 12.2 %fusion.7 = f32[512,512]{0,1:T(8,128)} fusion(f32[1024,512]{1,0:T(8,128)} %fusion, bf16[1024,2048]{1,0:T(8,128)(2,1)} %bitcast.50, bf16[1,2048,512]{2,1,0:T(8,128)(2,1)} %param.6), kind=kOutput, calls=%fused_computation.14 | convolution fusion | flops 2687500288 | bytes 9437184 | tf_op jit(solution)/shard_map/dot_general | solution.py:35
  145.6 39.2 %all-reduce.3.cloned.1.call-done = f32[512,512]{0,1:T(8,128)} async-done(((f32[512,512]{0,1:T(8,128)}), f32[512,512]{0,1:T(8,128)}) %all-reduce.3.cloned.1.call-update) | async-done | bytes 1048592 | tf_op jit(solution)/shard_map/psum | solution.py:41
  184.7 2.4 select_add_fusion
  187.1 2.6 copy.18
  189.7 1.5 fusion.9
  191.2 1.0 copy-done.3
  192.2 11.7 %cholesky.103 = f32[128,128]{1,0:T(8,128)S(1)} custom-call(f32[128,128]{1,0:T(8,128)S(1)} %cholesky.263), custom_call_target="Cholesky" | custom-call | tf_op jit(solution)/shard_map/jit(cholesky)/cholesky | solution.py:43
  203.9 10.0 %custom-call.27 = f32[1,128,128]{1,2,0:T(8,128)S(1)} custom-call(f32[1,128,128]{2,1,0:T(8,128)S(1)} %get-tuple-element.10), custom_call_target="InvertDiagBlocksLowerTriangular" | custom-call | tf_op jit(solution)/shard_map/jit(cholesky)/cholesky | solution.py:43
  214.0 1.2 fusion.15
  215.2 1.3 convolution_subtract_fusion
  216.5 11.7 %cholesky.215 = f32[128,128]{1,0:T(8,128)S(1)} custom-call(f32[128,128]{1,0:T(8,128)S(1)} %cholesky.267), custom_call_target="Cholesky" | custom-call | tf_op jit(solution)/shard_map/jit(cholesky)/cholesky | solution.py:43
  228.2 0.7 copy.21
  229.1 0.7 copy.19
  229.8 10.4 %custom-call.28 = f32[1,128,128]{1,2,0:T(8,128)} custom-call(f32[1,128,128]{2,1,0:T(8,128)S(1)} %get-tuple-element.8), custom_call_target="InvertDiagBlocksLowerTriangular" | custom-call | tf_op jit(solution)/shard_map/jit(cholesky)/cholesky | solution.py:43
  240.2 1.0 cholesky.222
  241.2 0.8 constant_dynamic-update-slice_fusion.2
  242.1 1.2 convolution_dynamic-update-slice_fusion
  243.2 1.5 convolution_subtract_fusion.1
  244.8 11.7 %cholesky.236 = f32[128,128]{1,0:T(8,128)S(1)} custom-call(f32[128,128]{1,0:T(8,128)S(1)} %cholesky.272), custom_call_target="Cholesky" | custom-call | tf_op jit(solution)/shard_map/jit(cholesky)/cholesky | solution.py:43
  256.6 10.0 %custom-call.29 = f32[1,128,128]{1,2,0:T(8,128)S(1)} custom-call(f32[1,128,128]{2,1,0:T(8,128)S(1)} %get-tuple-element.6), custom_call_target="InvertDiagBlocksLowerTriangular" | custom-call | tf_op jit(solution)/shard_map/jit(cholesky)/cholesky | solution.py:43
  266.9 1.3 convolution_subtract_fusion.2
  268.3 11.7 %cholesky.253 = f32[128,128]{1,0:T(8,128)S(1)} custom-call(f32[128,128]{1,0:T(8,128)S(1)} %convolution_subtract_fusion.2), custom_call_target="Cholesky" | custom-call | tf_op jit(solution)/shard_map/jit(cholesky)/cholesky | solution.py:43
  284.7 0.9 fusion.12
  (41 shorter events, 4.3 us)
Async XLA Ops:
  6.5 123.1 %copy-start = (bf16[1,2048,512]{2,1,0:T(8,128)(2,1)S(1)}, bf16[1,2048,512]{2,1,0:T(8,128)(2,1)}, u32[]{:S(2)}) copy-start(bf16[1,2048,512]{2,1,0:T(8,128)(2,1)} %param.7) | copy-start | bytes 6291460
  6.5 178.2 %all-reduce.3.cloned.1.call-start = ((), (), s32[]{:S(2)}) async-start(), calls=%async_computation.1 | async-start | bytes 2097152 | tf_op jit(solution)/shard_map/psum | solution.py:41
  127.7 1.9 copy-start.2
  184.7 5.0 %copy-start.1 = (f32[512,512]{0,1:T(8,128)S(1)}, f32[512,512]{0,1:T(8,128)}, u32[]{:S(2)}) copy-start(f32[512,512]{0,1:T(8,128)} %all-reduce.3.cloned.1.call-done) | copy-start | bytes 3145732
  191.2 1.0 copy-start.3
Sparse Core Ops, SparseCore 0:
  145.7 38.9 all-reduce.2
where the time goes:
time: 293 us; the launch traced here: 292 us
  blocking collectives  100 us (34%)
  other arithmetic  88.8 us (30%)
  waiting for transfers between devices  39.2 us (13%)
  local copies, waits for them, and re-layouts  25.6 us (9%)
  matrix products  22.7 us (8%)
  between operations  16.1 us (5%)
    all_to_all x1, blocking collectives, body(): lax.all_to_all(outbox, 'expert', split_axis=0, concat_axis=0, tiled=True)  100 us
    another operation x14, other arithmetic, body(): factor = jnp.linalg.cholesky(regular).T  79.4 us
    psum x1, waiting for transfers between devices, body(): summed = lax.psum(gram_local, 'dp')  39.2 us
    dot_general x1, matrix products, body(): lax.dot_general(hidden, hidden, (((0,), (0,)), ((), ())), preferred_eleme...  12.2 us
    gather x1, local copies, waits for them, and re-layouts, body(): tokens[source_row]  9.94 us
    another operation x6, matrix products, body(): factor = jnp.linalg.cholesky(regular).T  6.75 us
  transfers between devices with their start and end apart: 1, of which 1 were waited for; matrix products, arithmetic and copies ran while one was open for 0% of the time, Pallas kernels for 0%

commit v1 on v0

--- a/solution.py
+++ b/solution.py
@@ -38,7 +38,7 @@
     rows_mean = data_ranks * tok_rows * top_count
     block_rows = factor_width // data_ranks
     my_rank = lax.axis_index("dp")
-    summed = lax.psum(gram_local, "dp")
+    summed = jnp.sum(lax.all_gather(gram_local, "dp"), axis=0)
     regular = summed / rows_mean + RIDGE * jnp.eye(factor_width, dtype=jnp.float32)
     factor = jnp.linalg.cholesky(regular).T
     my_rows = lax.dynamic_slice_in_dim(factor, my_rank * block_rows, block_rows, 0)

time: 293 us -> 283 us (0.966)
  waiting for transfers between devices: 39.2 us -> 32.2 us
    psum x1 -> x0, waiting for transfers between devices: 39.2 us -> none  [body(): summed = lax.psum(gram_local, 'dp')]
    all_gather x0 -> x1, waiting for transfers between devices: none -> 32.2 us  [body(): summed = jnp.sum(lax.all_gather(gram_local, 'dp'), axis=0)]
    another operation x13 -> x4, local copies, waits for them, and re-layouts: 3.62 us -> 0.14 us  [body(): factor = jnp.linalg.cholesky(regular).T]
where the time goes in v1:
time: 283 us
  blocking collectives  100 us (35%)
  other arithmetic  88.7 us (31%)
  waiting for transfers between devices  32.2 us (11%)
  local copies, waits for them, and re-layouts  24.1 us (9%)
  matrix products  21.4 us (8%)
  between operations  16.2 us (6%)
    all_to_all x1, blocking collectives, body(): lax.all_to_all(outbox, 'expert', split_axis=0, concat_axis=0, tiled=True)  100 us
    another operation x14, other arithmetic, body(): factor = jnp.linalg.cholesky(regular).T  78.9 us
    all_gather x1, waiting for transfers between devices, body(): summed = jnp.sum(lax.all_gather(gram_local, 'dp'), axis=0)  32.2 us
    dot_general x1, matrix products, body(): lax.dot_general(hidden, hidden, (((0,), (0,)), ((), ())), preferred_eleme...  12.2 us
    gather x1, local copies, waits for them, and re-layouts, body(): tokens[source_row]  9.94 us
  transfers between devices with their start and end apart: 1, of which 1 were waited for; matrix products, arithmetic and copies ran while one was open for 0% of the time, Pallas kernels for 0%

profile of v1, /device:TPU:0, one launch (start us, length us, event | category | flops | bytes accessed | tf_op | source)
XLA Modules:
  0.0 282.7 jit_solution(14788520626387545739)
XLA Ops:
  6.5 0.9 copy.8
  7.7 0.7 broadcast_multiply_fusion
  8.4 1.1 reduce-window.6
  10.1 2.4 scatter_custom_fusion.1
  12.6 2.4 scatter_custom_fusion
  15.1 9.9 %gather_fusion = bf16[1024,2048]{1,0:T(8,128)(2,1)} fusion(bf16[128,2048]{1,0:T(8,128)(2,1)} %param.4, s32[1024]{0:T(1024)S(1)} %fusion.25), kind=kCustom, calls=%fused_computation | custom fusion | bytes 8392704 | tf_op jit(solution)/shard_map/gather | solution.py:24
  25.0 2.5 broadcast_select_fusion
  27.6 100.1 %all_to_all.5 = bf16[8,128,2048]{2,1,0:T(8,128)(2,1)S(1)} all-to-all(bf16[8,128,2048]{2,1,0:T(8,128)(2,1)S(1)} %broadcast_select_fusion), channel_id=1, replica_groups=mesh['groups'=2,'dp'=2,'expert'=8] {'expert'}, dimensions={0} | all-to-all | bytes 8388608 | tf_op jit(solution)/shard_map/all_to_all | solution.py:28
  127.7 1.9 copy-done.1
  129.6 3.7 %fusion = f32[1024,512]{1,0:T(8,128)} fusion(bf16[1024,2048]{1,0:T(8,128)(2,1)S(1)} %bitcast.50, bf16[1,2048,512]{2,1,0:T(8,128)(2,1)S(1)} %copy-done), kind=kOutput, calls=%fused_computation.4 | convolution fusion | flops 2147483648 | bytes 8388608 | tf_op jit(solution)/shard_map/dot_general | solution.py:31
  133.3 12.2 %fusion.7 = f32[512,512]{1,0:T(8,128)} fusion(f32[1024,512]{1,0:T(8,128)} %fusion, bf16[1024,2048]{1,0:T(8,128)(2,1)} %bitcast.51, bf16[1,2048,512]{2,1,0:T(8,128)(2,1)} %param.6), kind=kOutput, calls=%fused_computation.14 | convolution fusion | flops 2687500288 | bytes 9437184 | tf_op jit(solution)/shard_map/dot_general | solution.py:35
  145.6 32.2 %all-gather.3.cloned.1.call-done = f32[1024,512]{1,0:T(8,128)} async-done(((f32[512,512]{1,0:T(8,128)}), f32[1024,512]{1,0:T(8,128)}) %all-gather.3.cloned.1.call-update) | async-done | bytes 2097168 | tf_op jit(solution)/shard_map/all_gather | solution.py:41
  177.7 1.9 reduce_sum.19
  179.6 1.1 multiply_bitcast_fusion
  180.7 2.6 copy.10
  183.3 1.5 add_multiply_fusion
  184.8 1.0 copy-done.2
  185.8 11.7 %cholesky.103 = f32[128,128]{1,0:T(8,128)S(1)} custom-call(f32[128,128]{1,0:T(8,128)S(1)} %cholesky.263), custom_call_target="Cholesky" | custom-call | tf_op jit(solution)/shard_map/jit(cholesky)/cholesky | solution.py:43
  197.6 10.0 %custom-call.27 = f32[1,128,128]{1,2,0:T(8,128)S(1)} custom-call(f32[1,128,128]{2,1,0:T(8,128)S(1)} %get-tuple-element.14), custom_call_target="InvertDiagBlocksLowerTriangular" | custom-call | tf_op jit(solution)/shard_map/jit(cholesky)/cholesky | solution.py:43
  207.7 1.2 constant_dynamic-update-slice_fusion.3
  208.9 1.3 convolution_subtract_fusion
  210.2 11.7 %cholesky.215 = f32[128,128]{1,0:T(8,128)S(1)} custom-call(f32[128,128]{1,0:T(8,128)S(1)} %cholesky.267), custom_call_target="Cholesky" | custom-call | tf_op jit(solution)/shard_map/jit(cholesky)/cholesky | solution.py:43
  221.9 9.8 %custom-call.28 = f32[1,128,128]{1,2,0:T(8,128)S(1)} custom-call(f32[1,128,128]{2,1,0:T(8,128)S(1)} %get-tuple-element.11), custom_call_target="InvertDiagBlocksLowerTriangular" | custom-call | tf_op jit(solution)/shard_map/jit(cholesky)/cholesky | solution.py:43
  232.0 1.3 convolution_subtract_fusion.1
  233.3 11.7 %cholesky.236 = f32[128,128]{1,0:T(8,128)S(1)} custom-call(f32[128,128]{1,0:T(8,128)S(1)} %cholesky.272), custom_call_target="Cholesky" | custom-call | tf_op jit(solution)/shard_map/jit(cholesky)/cholesky | solution.py:43
  245.1 0.7 compare_reduce_fusion.1
  245.8 10.0 %custom-call.29 = f32[1,128,128]{1,2,0:T(8,128)S(1)} custom-call(f32[1,128,128]{2,1,0:T(8,128)S(1)} %get-tuple-element.8), custom_call_target="InvertDiagBlocksLowerTriangular" | custom-call | tf_op jit(solution)/shard_map/jit(cholesky)/cholesky | solution.py:43
  256.0 1.2 convolution_subtract_fusion.2
  257.2 11.7 %cholesky.253 = f32[128,128]{1,0:T(8,128)S(1)} custom-call(f32[128,128]{1,0:T(8,128)S(1)} %convolution_subtract_fusion.2), custom_call_target="Cholesky" | custom-call | tf_op jit(solution)/shard_map/jit(cholesky)/cholesky | solution.py:43
  269.0 0.7 compare_reduce_fusion
  272.9 0.9 fusion.11
  273.8 2.0 copy.11
  (32 shorter events, 2.2 us)
Async XLA Ops:
  6.5 123.1 %copy-start = (bf16[1,2048,512]{2,1,0:T(8,128)(2,1)S(1)}, bf16[1,2048,512]{2,1,0:T(8,128)(2,1)}, u32[]{:S(2)}) copy-start(bf16[1,2048,512]{2,1,0:T(8,128)(2,1)} %param.7) | copy-start | bytes 6291460
  6.5 171.2 %all-gather.3.cloned.1.call-start = ((), (), s32[]{:S(2)}) async-start(), calls=%async_computation.1 | async-start | bytes 3145728 | tf_op jit(solution)/shard_map/all_gather | solution.py:41
  127.7 1.9 copy-start.1
  184.8 1.0 copy-start.2
Sparse Core Ops, SparseCore 0:
  145.7 32.0 all-gather.2
